TPU v7x, 32 devices: a whole 2x2x4 slice. The times are simulated.
32 devices in a mesh: groups: 2 (over y), row: 4 (over z), col: 2 (over x), rep: 2 (over core).
Axes of the slice: x: 2, y: 2, z: 4, core: 2. Of those that a mesh axis runs over, the one named last changes fastest.
Arguments:
- kernel: float32 [32768, 16384], P(('groups', 'row'), ('col', 'rep')), parts along dimension 0, may hold values from 0 to 2, as said below
- source: float32 [64, 16384], P('groups', 'row'), parts along dimension 0, may hold values from 0.5 to 2, as said below
- target: float32 [64, 16384], P('groups', ('col', 'rep')), parts along dimension 0, may hold values from 0.5 to 2, as said below
Outputs:
- left_scale: float32 [64, 16384], P('groups', 'row'), parts along dimension 0
- right_scale: float32 [64, 16384], P('groups', ('col', 'rep')), parts along dimension 0
- errors: float32 [6, 32], P('groups'), parts along dimension 0
There are 2 independent parts, one for each index of `groups`. A program takes and returns all parts, laid end to end along the dimension named above; each array names one. Nothing has to cross between parts.
Inputs may be any that keep to these rules, and one draw needn't show every extreme that they name: `kernel`: every entry is positive. `source`: every entry is positive. `target`: every entry is positive.
All inputs are finite; a program needn't handle non-finite values.
Results may differ from a plain program's by a relative error of at most 0.0001.
Values sent between devices are 32-bit elements; how exact they have to be, the bound alone decides.
A program may use at most 128 MiB of HBM per device.

v0:
```python
import jax
import jax.numpy as jnp
from jax import lax
from jax.sharding import PartitionSpec as P

N = 16384
ITERS = 3


def local(kernel, source, target):
    columns = kernel.shape[1]
    right_scale = jnp.ones(target.shape, jnp.float32)
    left_scale = source
    share = columns // lax.axis_size("row")
    offset = lax.axis_index("row") * share
    errors = []
    for step in range(ITERS):
        partial_value = lax.dot_general(
            right_scale, kernel, (((1,), (1,)), ((), ())), precision=lax.Precision.HIGHEST
        )
        left_scale = source / lax.psum(partial_value, ("col", "rep"))
        back = jnp.dot(left_scale, kernel, precision=lax.Precision.HIGHEST)
        old_piece = lax.dynamic_slice_in_dim(right_scale, offset, share, 1)
        target_piece = lax.dynamic_slice_in_dim(target, offset, share, 1)
        total_piece = lax.psum_scatter(back, "row", scatter_dimension=1, tiled=True)
        right_scale = lax.all_gather(target_piece / total_piece, "row", axis=1, tiled=True)
        term = jnp.sum(jnp.abs(old_piece * total_piece - target_piece), axis=1) / N
        errors.append(lax.psum(term, ("row", "col", "rep")))
    stacked = jnp.stack(errors)
    return (left_scale, right_scale, stacked)


def solution(mesh):
    return jax.shard_map(
        local,
        mesh=mesh,
        in_specs=(
            P(("groups", "row"), ("col", "rep")),
            P("groups", "row"),
            P("groups", ("col", "rep")),
        ),
        out_specs=(P("groups", "row"), P("groups", ("col", "rep")), P("groups", None)),
        check_vma=False,
    )
```

profile of v0, /device:TPU:0, one launch (start us, length us, event | category | flops | bytes accessed | tf_op | source)
XLA Modules:
  0.0 597.1 jit_solution(12538912805392526422)
XLA Ops:
  7.2 66.4 %fusion.4 = f32[32,4096]{1,0:T(8,128)} fusion(f32[4096,4096]{1,0:T(8,128)} %param.3), kind=kOutput, calls=%fused_computation.4 | convolution fusion | flops 6442450944 | bytes 67633152 | tf_op jit(solution)/shard_map/dot_general | solution.py:18
  73.7 0.3 reduce-scatter.4.cloned.1.call-start
  74.0 36.0 %all-reduce.5.cloned.1.call-done = f32[32,4096]{1,0:T(8,128)} async-done(((f32[32,4096]{1,0:T(8,128)}), f32[32,4096]{1,0:T(8,128)}) %all-reduce.5.cloned.1.call-update) | async-done | bytes 524304 | tf_op jit(solution)/shard_map/psum | solution.py:21
  110.0 44.8 %fusion.2 = f32[32,4096]{1,0:T(8,128)} fusion(f32[4096,4096]{1,0:T(8,128)} %param.3, f32[32,4096]{1,0:T(8,128)S(1)} %copy-done, f32[32,4096]{1,0:T(8,128)} %all-reduce.5.cloned.1.call-done), kind=kOutput, calls=%fused_computation.2 | convolution fusion | flops 6442582016 | bytes 68681728 | tf_op jit(solution)/shard_map/dot_general | solution.py:22
  154.9 22.1 %reduce-scatter.4.cloned.1.call-done = f32[32,1024]{1,0:T(8,128)} async-done(((f32[32,4096]{1,0:T(8,128)}), f32[32,1024]{1,0:T(8,128)}) %reduce-scatter.4.cloned.1.call-update) | async-done | bytes 131088 | tf_op jit(solution)/shard_map/reduce_scatter | solution.py:25
  177.0 0.9 dynamic-slice_divide_fusion.2
  177.9 15.7 %all_gather.9 = f32[32,4096]{1,0:T(8,128)S(1)} all-gather(f32[32,1024]{1,0:T(8,128)S(1)} %dynamic-slice_divide_fusion.2), channel_id=1, replica_groups=mesh['groups'=2,'row'=4,'col'=2,'rep'=2] {'row'}, dimensions={1}, use_global_device_ids=true | all-gather | bytes 655360 | tf_op jit(solution)/shard_map/all_gather | solution.py:26
  193.7 66.5 %fusion.7 = f32[32,4096]{1,0:T(8,128)} fusion(f32[32,4096]{1,0:T(8,128)S(1)} %all_gather.9, f32[4096,4096]{1,0:T(8,128)} %param.3), kind=kOutput, calls=%fused_computation.17 | convolution fusion | flops 6442450944 | bytes 68157440 | tf_op jit(solution)/shard_map/dot_general | solution.py:18
  260.4 31.8 %all-reduce.7.cloned.1.call-done = f32[32,4096]{1,0:T(8,128)} async-done(((f32[32,4096]{1,0:T(8,128)}), f32[32,4096]{1,0:T(8,128)}) %all-reduce.7.cloned.1.call-update) | async-done | bytes 524304 | tf_op jit(solution)/shard_map/psum | solution.py:21
  292.2 44.8 %fusion = f32[32,4096]{1,0:T(8,128)} fusion(f32[4096,4096]{1,0:T(8,128)} %param.3, f32[32,4096]{1,0:T(8,128)S(1)} %copy-done, f32[32,4096]{1,0:T(8,128)} %all-reduce.7.cloned.1.call-done), kind=kOutput, calls=%fused_computation | convolution fusion | flops 6442582016 | bytes 68681728 | tf_op jit(solution)/shard_map/dot_general | solution.py:22
  337.1 22.0 %reduce-scatter.6.cloned.1.call-done = f32[32,1024]{1,0:T(8,128)} async-done(((f32[32,4096]{1,0:T(8,128)}), f32[32,1024]{1,0:T(8,128)}) %reduce-scatter.6.cloned.1.call-update) | async-done | bytes 131088 | tf_op jit(solution)/shard_map/reduce_scatter | solution.py:25
  359.1 0.9 dynamic-slice_divide_fusion.1
  360.0 15.7 %all_gather.10 = f32[32,4096]{1,0:T(8,128)S(1)} all-gather(f32[32,1024]{1,0:T(8,128)S(1)} %dynamic-slice_divide_fusion.1), channel_id=1, replica_groups=mesh['groups'=2,'row'=4,'col'=2,'rep'=2] {'row'}, dimensions={1}, use_global_device_ids=true | all-gather | bytes 655360 | tf_op jit(solution)/shard_map/all_gather | solution.py:26
  375.7 66.5 %fusion.8 = f32[32,4096]{1,0:T(8,128)} fusion(f32[32,4096]{1,0:T(8,128)S(1)} %all_gather.10, f32[4096,4096]{1,0:T(8,128)} %param.3), kind=kOutput, calls=%fused_computation.18 | convolution fusion | flops 6442450944 | bytes 68157440 | tf_op jit(solution)/shard_map/dot_general | solution.py:18
  442.2 0.3 reduce-scatter.8.cloned.1.call-start
  442.5 31.6 %all-reduce.9.cloned.1.call-done = f32[32,4096]{1,0:T(8,128)} async-done(((f32[32,4096]{1,0:T(8,128)}), f32[32,4096]{1,0:T(8,128)}) %all-reduce.9.cloned.1.call-update) | async-done | bytes 524304 | tf_op jit(solution)/shard_map/psum | solution.py:21
  474.2 1.1 div.31
  475.3 45.0 %fusion.9 = f32[32,4096]{1,0:T(8,128)} fusion(f32[32,4096]{1,0:T(8,128)S(1)} %div.31, f32[4096,4096]{1,0:T(8,128)} %param.3), kind=kOutput, calls=%fused_computation.19 | convolution fusion | flops 6442450944 | bytes 68157440 | tf_op jit(solution)/shard_map/dot_general | solution.py:22
  520.4 22.1 %reduce-scatter.8.cloned.1.call-done = f32[32,1024]{1,0:T(8,128)} async-done(((f32[32,4096]{1,0:T(8,128)}), f32[32,1024]{1,0:T(8,128)}) %reduce-scatter.8.cloned.1.call-update) | async-done | bytes 131088 | tf_op jit(solution)/shard_map/reduce_scatter | solution.py:25
  542.5 1.1 abs_reduce_fusion.2
  543.6 15.3 %all_gather.11 = f32[32,4096]{1,0:T(8,128)S(1)} all-gather(f32[32,1024]{1,0:T(8,128)S(1)} %get-tuple-element.9), channel_id=1, replica_groups=mesh['groups'=2,'row'=4,'col'=2,'rep'=2] {'row'}, dimensions={1}, use_global_device_ids=true | all-gather | bytes 655360 | tf_op jit(solution)/shard_map/all_gather | solution.py:26
  558.9 29.5 %all-reduce = (f32[1,32]{1,0:T(1,128)S(1)}, f32[1,32]{1,0:T(1,128)S(1)}, f32[1,32]{1,0:T(1,128)S(1)}) all-reduce(f32[1,32]{1,0:T(1,128)S(1)} %get-tuple-element.10, f32[1,32]{1,0:T(1,128)S(1)} %get-tuple-element.11, f32[1,32]{1,0:T(1,128)S(1)} %multiply_bitcast_fusion.2), channel_id=1, replica_groups=mesh['groups'=2,'row'=4,'col'=2,'rep'=2] {'row','col','rep'}, use_global_device_ids=true, to_apply=%region_11.0 | all-reduce | flops 96 | bytes 768 | tf_op jit(solution)/shard_map/psum | solution.py:28
  588.4 0.6 pad_maximum_fusion
  589.0 0.8 copy.10
  (22 shorter events, 0.5 us)
Async XLA Ops:
  7.2 102.8 %copy-start = (f32[32,4096]{1,0:T(8,128)S(1)}, f32[32,4096]{1,0:T(8,128)}, u32[]{:S(2)}) copy-start(f32[32,4096]{1,0:T(8,128)} %param.4) | copy-start | bytes 1572868
  7.2 102.8 %all-reduce.5.cloned.1.call-start = ((), (), s32[]{:S(2)}) async-start(), calls=%async_computation.3 | async-start | bytes 1048576 | tf_op jit(solution)/shard_map/psum | solution.py:21
  73.7 103.3 %copy-start.4 = (f32[32,4096]{1,0:T(8,128)S(1)}, f32[32,4096]{1,0:T(8,128)}, u32[]{:S(2)}) copy-start(f32[32,4096]{1,0:T(8,128)} %param.5) | copy-start | bytes 1572868
  73.7 103.3 %reduce-scatter.4.cloned.1.call-start = ((), (), s32[]{:S(2)}) async-start(), calls=%async_computation.4 | async-start | bytes 655360 | tf_op jit(solution)/shard_map/reduce_scatter | solution.py:25
  154.9 137.3 %all-reduce.7.cloned.1.call-start = ((), (), s32[]{:S(2)}) async-start(), calls=%async_computation.5 | async-start | bytes 1048576 | tf_op jit(solution)/shard_map/psum | solution.py:21
  260.2 98.9 %reduce-scatter.6.cloned.1.call-start = ((), (), s32[]{:S(2)}) async-start(), calls=%async_computation.6 | async-start | bytes 655360 | tf_op jit(solution)/shard_map/reduce_scatter | solution.py:25
  337.0 137.1 %all-reduce.9.cloned.1.call-start = ((), (), s32[]{:S(2)}) async-start(), calls=%async_computation.7 | async-start | bytes 1048576 | tf_op jit(solution)/shard_map/psum | solution.py:21
  442.2 100.3 %copy-start.2 = (f32[32,1024]{1,0:T(8,128)S(1)}, f32[32,1024]{1,0:T(8,128)}, u32[]{:S(2)}) copy-start(f32[32,1024]{1,0:T(8,128)} %reduce-scatter.4.cloned.1.call-done) | copy-start | bytes 393220
  442.2 100.3 %copy-start.3 = (f32[32,1024]{1,0:T(8,128)S(1)}, f32[32,1024]{1,0:T(8,128)}, u32[]{:S(2)}) copy-start(f32[32,1024]{1,0:T(8,128)} %reduce-scatter.6.cloned.1.call-done) | copy-start | bytes 393220
  442.2 100.2 %reduce-scatter.8.cloned.1.call-start = ((), (), s32[]{:S(2)}) async-start(), calls=%async_computation.8 | async-start | bytes 655360 | tf_op jit(solution)/shard_map/reduce_scatter | solution.py:25
  475.3 114.5 %copy-start.1 = (f32[32,4096]{1,0:T(8,128)}, f32[32,4096]{1,0:T(8,128)S(1)}, u32[]{:S(2)}) copy-start(f32[32,4096]{1,0:T(8,128)S(1)} %div.31) | copy-start | bytes 1572868
Sparse Core Ops, SparseCore 0:
  73.8 36.1 all-reduce.4
  155.0 21.9 reduce-scatter.3
  260.3 31.8 all-reduce.6
  337.1 21.9 reduce-scatter.5
  442.4 31.7 all-reduce.8
  520.5 21.9 reduce-scatter.7
where the time goes:
time: 606 us; the launch traced here: 597 us
  matrix products  334 us (55%)
  waiting for transfers between devices  166 us (27%)
  blocking collectives  76.2 us (13%)
  between operations  14.6 us (2%)
    dot_general x3, matrix products, local(): lax.dot_general(right_scale, kernel, (((1,), (1,)), ((), ())), precision=...  199 us
    dot_general x3, matrix products, local(): back = jnp.dot(left_scale, kernel, precision=lax.Precision.HIGHEST)  135 us
    psum x3, waiting for transfers between devices, local(): left_scale = source / lax.psum(partial_value, ('col', 'rep'))  99.4 us
    reduce_scatter x3, waiting for transfers between devices, local(): total_piece = lax.psum_scatter(back, 'row', scatter_dimension=1, tiled=True)  66.2 us
    all_gather x3, blocking collectives, local(): lax.all_gather(target_piece / total_piece, 'row', axis=1, tiled=True)  46.8 us
    psum x1, blocking collectives, local(): errors.append(lax.psum(term, ('row', 'col', 'rep')))  29.5 us
  transfers between devices with their start and end apart: 6, of which 6 were waited for; matrix products, arithmetic and copies ran while one was open for 0% of the time, Pallas kernels for 0%

commit v1 on v0

--- a/solution.py
+++ b/solution.py
@@ -23,7 +23,9 @@
         old_piece = lax.dynamic_slice_in_dim(right_scale, offset, share, 1)
         target_piece = lax.dynamic_slice_in_dim(target, offset, share, 1)
         total_piece = lax.psum_scatter(back, "row", scatter_dimension=1, tiled=True)
-        right_scale = lax.all_gather(target_piece / total_piece, "row", axis=1, tiled=True)
+        block = target_piece / total_piece
+        blocks = lax.all_gather(block, "row")
+        right_scale = jnp.concatenate(blocks, axis=1)
         term = jnp.sum(jnp.abs(old_piece * total_piece - target_piece), axis=1) / N
         errors.append(lax.psum(term, ("row", "col", "rep")))
     stacked = jnp.stack(errors)

time: 606 us -> 607 us (level)
  no operation moved by 1% of the time
where the time goes in v1:
time: 607 us; the launch traced here: 599 us
  matrix products  335 us (55%)
  waiting for transfers between devices  166 us (27%)
  blocking collectives  75.5 us (12%)
  between operations  14.6 us (2%)
    dot_general x3, matrix products, local(): lax.dot_general(right_scale, kernel, (((1,), (1,)), ((), ())), precision=...  200 us
    dot_general x3, matrix products, local(): back = jnp.dot(left_scale, kernel, precision=lax.Precision.HIGHEST)  135 us
    psum x3, waiting for transfers between devices, local(): left_scale = source / lax.psum(partial_value, ('col', 'rep'))  99.9 us
    reduce_scatter x3, waiting for transfers between devices, local(): total_piece = lax.psum_scatter(back, 'row', scatter_dimension=1, tiled=True)  66.2 us
    all_gather x3, blocking collectives, local(): blocks = lax.all_gather(block, 'row')  46 us
    psum x1, blocking collectives, local(): errors.append(lax.psum(term, ('row', 'col', 'rep')))  29.5 us
  transfers between devices with their start and end apart: 6, of which 6 were waited for; matrix products, arithmetic and copies ran while one was open for 0% of the time, Pallas kernels for 0%

profile of v1, /device:TPU:0, one launch (start us, length us, event | category | flops | bytes accessed | tf_op | source)
XLA Modules:
  0.0 598.6 jit_solution(3108128837993985100)
XLA Ops:
  7.2 66.4 %fusion.4 = f32[32,4096]{1,0:T(8,128)} fusion(f32[4096,4096]{1,0:T(8,128)} %param.3), kind=kOutput, calls=%fused_computation.4 | convolution fusion | flops 6442450944 | bytes 67633152 | tf_op jit(solution)/shard_map/dot_general | solution.py:18
  74.0 36.0 %all-reduce.5.cloned.1.call-done = f32[32,4096]{1,0:T(8,128)} async-done(((f32[32,4096]{1,0:T(8,128)}), f32[32,4096]{1,0:T(8,128)}) %all-reduce.5.cloned.1.call-update) | async-done | bytes 524304 | tf_op jit(solution)/shard_map/psum | solution.py:21
  110.0 44.8 %fusion.2 = f32[32,4096]{1,0:T(8,128)} fusion(f32[4096,4096]{1,0:T(8,128)} %param.3, f32[32,4096]{1,0:T(8,128)S(1)} %copy-done, f32[32,4096]{1,0:T(8,128)} %all-reduce.5.cloned.1.call-done), kind=kOutput, calls=%fused_computation.2 | convolution fusion | flops 6442582016 | bytes 68681728 | tf_op jit(solution)/shard_map/dot_general | solution.py:22
  154.9 22.1 %reduce-scatter.4.cloned.1.call-done = f32[32,1024]{1,0:T(8,128)} async-done(((f32[32,4096]{1,0:T(8,128)}), f32[32,1024]{1,0:T(8,128)}) %reduce-scatter.4.cloned.1.call-update) | async-done | bytes 131088 | tf_op jit(solution)/shard_map/reduce_scatter | solution.py:25
  177.0 0.9 dynamic-slice_divide_fusion.2
  177.9 15.3 %all-gather = f32[128,1024]{1,0:T(8,128)S(1)} all-gather(f32[32,1024]{1,0:T(8,128)S(1)} %dynamic-slice_divide_fusion.2), channel_id=2, replica_groups=mesh['groups'=2,'row'=4,'col'=2,'rep'=2] {'row'}, dimensions={0}, use_global_device_ids=true | all-gather | bytes 655360 | tf_op jit(solution)/shard_map/all_gather | solution.py:27
  193.3 0.3 copy.6
  193.9 66.9 %fusion.7 = f32[32,4096]{1,0:T(8,128)} fusion(f32[32,4096]{1,0:T(8,128)S(1)} %bitcast.28, f32[4096,4096]{1,0:T(8,128)} %param.3), kind=kOutput, calls=%fused_computation.17 | convolution fusion | flops 6442450944 | bytes 68157440 | tf_op jit(solution)/shard_map/dot_general | solution.py:18
  260.9 31.9 %all-reduce.7.cloned.1.call-done = f32[32,4096]{1,0:T(8,128)} async-done(((f32[32,4096]{1,0:T(8,128)}), f32[32,4096]{1,0:T(8,128)}) %all-reduce.7.cloned.1.call-update) | async-done | bytes 524304 | tf_op jit(solution)/shard_map/psum | solution.py:21
  292.8 45.0 %fusion = f32[32,4096]{1,0:T(8,128)} fusion(f32[4096,4096]{1,0:T(8,128)} %param.3, f32[32,4096]{1,0:T(8,128)S(1)} %copy-done, f32[32,4096]{1,0:T(8,128)} %all-reduce.7.cloned.1.call-done), kind=kOutput, calls=%fused_computation | convolution fusion | flops 6442582016 | bytes 68681728 | tf_op jit(solution)/shard_map/dot_general | solution.py:22
  337.9 22.1 %reduce-scatter.6.cloned.1.call-done = f32[32,1024]{1,0:T(8,128)} async-done(((f32[32,4096]{1,0:T(8,128)}), f32[32,1024]{1,0:T(8,128)}) %reduce-scatter.6.cloned.1.call-update) | async-done | bytes 131088 | tf_op jit(solution)/shard_map/reduce_scatter | solution.py:25
  360.0 0.9 dynamic-slice_divide_fusion.1
  360.9 15.3 %all-gather.1 = f32[128,1024]{1,0:T(8,128)S(1)} all-gather(f32[32,1024]{1,0:T(8,128)S(1)} %dynamic-slice_divide_fusion.1), channel_id=3, replica_groups=mesh['groups'=2,'row'=4,'col'=2,'rep'=2] {'row'}, dimensions={0}, use_global_device_ids=true | all-gather | bytes 655360 | tf_op jit(solution)/shard_map/all_gather | solution.py:27
  376.2 0.3 copy.7
  376.9 66.7 %fusion.8 = f32[32,4096]{1,0:T(8,128)} fusion(f32[32,4096]{1,0:T(8,128)S(1)} %bitcast.30, f32[4096,4096]{1,0:T(8,128)} %param.3), kind=kOutput, calls=%fused_computation.18 | convolution fusion | flops 6442450944 | bytes 68157440 | tf_op jit(solution)/shard_map/dot_general | solution.py:18
  443.7 31.9 %all-reduce.9.cloned.1.call-done = f32[32,4096]{1,0:T(8,128)} async-done(((f32[32,4096]{1,0:T(8,128)}), f32[32,4096]{1,0:T(8,128)}) %all-reduce.9.cloned.1.call-update) | async-done | bytes 524304 | tf_op jit(solution)/shard_map/psum | solution.py:21
  475.6 1.1 div.31
  476.8 45.1 %fusion.9 = f32[32,4096]{1,0:T(8,128)} fusion(f32[32,4096]{1,0:T(8,128)S(1)} %div.31, f32[4096,4096]{1,0:T(8,128)} %param.3), kind=kOutput, calls=%fused_computation.19 | convolution fusion | flops 6442450944 | bytes 68157440 | tf_op jit(solution)/shard_map/dot_general | solution.py:22
  521.9 22.1 %reduce-scatter.8.cloned.1.call-done = f32[32,1024]{1,0:T(8,128)} async-done(((f32[32,4096]{1,0:T(8,128)}), f32[32,1024]{1,0:T(8,128)}) %reduce-scatter.8.cloned.1.call-update) | async-done | bytes 131088 | tf_op jit(solution)/shard_map/reduce_scatter | solution.py:25
  544.0 1.1 abs_reduce_fusion.2
  545.1 15.3 %all-gather.2 = f32[128,1024]{1,0:T(8,128)S(1)} all-gather(f32[32,1024]{1,0:T(8,128)S(1)} %get-tuple-element.9), channel_id=4, replica_groups=mesh['groups'=2,'row'=4,'col'=2,'rep'=2] {'row'}, dimensions={0}, use_global_device_ids=true | all-gather | bytes 655360 | tf_op jit(solution)/shard_map/all_gather | solution.py:27
  560.5 0.8 copy.9
  561.3 29.5 %all-reduce = (f32[1,32]{1,0:T(1,128)S(1)}, f32[1,32]{1,0:T(1,128)S(1)}, f32[1,32]{1,0:T(1,128)S(1)}) all-reduce(f32[1,32]{1,0:T(1,128)S(1)} %get-tuple-element.10, f32[1,32]{1,0:T(1,128)S(1)} %get-tuple-element.11, f32[1,32]{1,0:T(1,128)S(1)} %multiply_bitcast_fusion.2), channel_id=1, replica_groups=mesh['groups'=2,'row'=4,'col'=2,'rep'=2] {'row','col','rep'}, use_global_device_ids=true, to_apply=%region_11.0 | all-reduce | flops 96 | bytes 768 | tf_op jit(solution)/shard_map/psum | solution.py:30
  590.8 0.6 pad_maximum_fusion
  (26 shorter events, 1.2 us)
Async XLA Ops:
  7.2 102.8 %copy-start = (f32[32,4096]{1,0:T(8,128)S(1)}, f32[32,4096]{1,0:T(8,128)}, u32[]{:S(2)}) copy-start(f32[32,4096]{1,0:T(8,128)} %param.4) | copy-start | bytes 1572868
  7.2 102.8 %all-reduce.5.cloned.1.call-start = ((), (), s32[]{:S(2)}) async-start(), calls=%async_computation.3 | async-start | bytes 1048576 | tf_op jit(solution)/shard_map/psum | solution.py:21
  73.7 103.3 %copy-start.4 = (f32[32,4096]{1,0:T(8,128)S(1)}, f32[32,4096]{1,0:T(8,128)}, u32[]{:S(2)}) copy-start(f32[32,4096]{1,0:T(8,128)} %param.5) | copy-start | bytes 1572868
  73.7 103.3 %reduce-scatter.4.cloned.1.call-start = ((), (), s32[]{:S(2)}) async-start(), calls=%async_computation.4 | async-start | bytes 655360 | tf_op jit(solution)/shard_map/reduce_scatter | solution.py:25
  154.9 138.0 %all-reduce.7.cloned.1.call-start = ((), (), s32[]{:S(2)}) async-start(), calls=%async_computation.5 | async-start | bytes 1048576 | tf_op jit(solution)/shard_map/psum | solution.py:21
  260.9 99.1 %reduce-scatter.6.cloned.1.call-start = ((), (), s32[]{:S(2)}) async-start(), calls=%async_computation.6 | async-start | bytes 655360 | tf_op jit(solution)/shard_map/reduce_scatter | solution.py:25
  337.9 137.8 %all-reduce.9.cloned.1.call-start = ((), (), s32[]{:S(2)}) async-start(), calls=%async_computation.7 | async-start | bytes 1048576 | tf_op jit(solution)/shard_map/psum | solution.py:21
  443.6 100.4 %copy-start.2 = (f32[32,1024]{1,0:T(8,128)S(1)}, f32[32,1024]{1,0:T(8,128)}, u32[]{:S(2)}) copy-start(f32[32,1024]{1,0:T(8,128)} %reduce-scatter.4.cloned.1.call-done) | copy-start | bytes 393220
  443.6 100.4 %copy-start.3 = (f32[32,1024]{1,0:T(8,128)S(1)}, f32[32,1024]{1,0:T(8,128)}, u32[]{:S(2)}) copy-start(f32[32,1024]{1,0:T(8,128)} %reduce-scatter.6.cloned.1.call-done) | copy-start | bytes 393220
  443.6 100.3 %reduce-scatter.8.cloned.1.call-start = ((), (), s32[]{:S(2)}) async-start(), calls=%async_computation.8 | async-start | bytes 655360 | tf_op jit(solution)/shard_map/reduce_scatter | solution.py:25
  476.7 114.6 %copy-start.1 = (f32[32,4096]{1,0:T(8,128)}, f32[32,4096]{1,0:T(8,128)S(1)}, u32[]{:S(2)}) copy-start(f32[32,4096]{1,0:T(8,128)S(1)} %div.31) | copy-start | bytes 1572868
Sparse Core Ops, SparseCore 0:
  73.8 36.1 all-reduce.4
  155.0 21.9 reduce-scatter.3
  261.0 31.8 all-reduce.6
  338.0 21.9 reduce-scatter.5
  443.8 31.8 all-reduce.8
  522.0 21.9 reduce-scatter.7
